TPU v7x, 32 devices: a whole 2x2x4 slice. The times are simulated.
32 devices in a mesh: gx: 2 (over core), gy: 16 (over z, y, x).
Axes of the slice: x: 2, y: 2, z: 4, core: 2. Of those that a mesh axis runs over, the one named last changes fastest.
Arguments:
- state: float32 [8, 2, 256, 256], P(None, None, 'gy', 'gx'), as said below
- offsets: int32 [2], replicated, may hold values from 0 to 255
Outputs:
- updated: float32 [8, 2, 256, 256], P(None, None, 'gy', 'gx')
Inputs may be any that keep to these rules, and one draw needn't show every extreme that they name: `state`: density lies in [0.5, 2]; each momentum over density differs from the background (0 for x and z, -1.5 x_i for y with x_i = (i + 0.5)/256 - 0.5) by at most 0.3; face fields lie in [-0.5, 0.5]; energy exceeds kinetic plus cell-centred magnetic energy by a pressure of 0.5 to 1.5 over (5/3 - 1).
All inputs are finite; a program needn't handle non-finite values.
Results may differ from a plain program's by a relative error of at most 0.00002.
Values sent between devices are 32-bit elements; how exact they have to be, the bound alone decides.
A program may use at most 64 MiB of HBM per device.

v0:
```python
import jax
import jax.numpy as jnp
from jax import lax
from jax.sharding import PartitionSpec as P

ADIABATIC = 5.0 / 3.0
SIGNAL_SPEED = 4.0
COURANT_RATIO = 0.06
SHEAR_SPEED = 1.5


def passed_along(block, axis, distance):
    devices = range(lax.axis_size(axis))
    route = [((i - distance) % len(devices), i) for i in devices]
    return lax.ppermute(block, axis, route)


def with_halo(block, sides, width):
    for axis, dim in sides:
        count = lax.axis_size(axis)
        forward = [(i, i + 1) for i in range(count - 1)]
        forward.append((count - 1, 0))
        backward = [(target, source) for source, target in forward]
        low = lax.ppermute(
            lax.slice_in_dim(block, block.shape[dim] - width, None, axis=dim), axis, forward
        )
        high = lax.ppermute(lax.slice_in_dim(block, 0, width, axis=dim), axis, backward)
        block = jnp.concatenate([low, block, high], axis=dim)
    return block


def physical_flux(conserved, direction):
    density = conserved[0]
    momenta = conserved[1:4]
    energy = conserved[4]
    magnetic = conserved[5:8]
    velocity = momenta / density
    magnetic_sq = jnp.sum(magnetic * magnetic, axis=0)
    pressure = (ADIABATIC - 1.0) * (
        energy - 0.5 * jnp.sum(momenta * velocity, axis=0) - 0.5 * magnetic_sq
    )
    total_pressure = pressure + 0.5 * magnetic_sq
    normal_speed = velocity[direction]
    normal_field = magnetic[direction]
    selector = (jnp.arange(3) == direction).astype(conserved.dtype)[:, None, None, None]
    momentum_flux = momenta * normal_speed - magnetic * normal_field + selector * total_pressure
    energy_flux = (energy + total_pressure) * normal_speed - normal_field * jnp.sum(
        velocity * magnetic, axis=0
    )
    induction = normal_speed * magnetic - velocity * normal_field
    return jnp.concatenate(
        [momenta[direction][None], momentum_flux, energy_flux[None], induction], axis=0
    )


def advance(padded):
    centre_x = 0.5 * (padded[5, :, 1:-1, 1:-1] + padded[5, :, 1:-1, 2:])
    centre_y = 0.5 * (padded[6, :, 1:-1, 1:-1] + padded[6, :, 2:, 1:-1])
    centre_z = 0.5 * (padded[7, :, 1:-1, 1:-1] + jnp.roll(padded[7], -1, axis=0)[:, 1:-1, 1:-1])
    conserved = jnp.concatenate(
        [padded[0:5, :, 1:-1, 1:-1], jnp.stack([centre_x, centre_y, centre_z])], axis=0
    )
    flux_phys = physical_flux(conserved, 0)
    face_x = 0.5 * (flux_phys[..., :-1] + flux_phys[..., 1:]) - 0.5 * SIGNAL_SPEED * (
        conserved[..., 1:] - conserved[..., :-1]
    )
    flux_phys = physical_flux(conserved, 1)
    face_y = 0.5 * (flux_phys[:, :, :-1] + flux_phys[:, :, 1:]) - 0.5 * SIGNAL_SPEED * (
        conserved[:, :, 1:] - conserved[:, :, :-1]
    )
    flux_phys = physical_flux(conserved, 2)
    face_z = 0.5 * (jnp.roll(flux_phys, 1, axis=1) + flux_phys) - 0.5 * SIGNAL_SPEED * (
        conserved - jnp.roll(conserved, 1, axis=1)
    )
    divergence = (
        face_x[:5, :, 1:-1, 1:]
        - face_x[:5, :, 1:-1, :-1]
        + (face_y[:5, :, 1:, 1:-1] - face_y[:5, :, :-1, 1:-1])
    )
    divergence = divergence + (jnp.roll(face_z[:5], -1, axis=1) - face_z[:5])[:, :, 1:-1, 1:-1]
    hydro = padded[0:5, :, 2:-2, 2:-2] - COURANT_RATIO * divergence
    emf_z = 0.25 * (
        -(face_x[6, :, 1:, :] + face_x[6, :, :-1, :]) + (face_y[5, :, :, 1:] + face_y[5, :, :, :-1])
    )
    emf_x = 0.25 * (
        -(face_y[7] + jnp.roll(face_y[7], 1, axis=0)) + (face_z[6, :, 1:, :] + face_z[6, :, :-1, :])
    )
    emf_y = 0.25 * (
        face_x[7] + jnp.roll(face_x[7], 1, axis=0) - (face_z[5, :, :, 1:] + face_z[5, :, :, :-1])
    )
    new_bx = padded[5, :, 2:-2, 2:-2] - COURANT_RATIO * (
        emf_z[:, 1:, :-1] - emf_z[:, :-1, :-1] - (jnp.roll(emf_y, -1, axis=0) - emf_y)[:, 1:-1, :-1]
    )
    new_by = padded[6, :, 2:-2, 2:-2] - COURANT_RATIO * (
        (jnp.roll(emf_x, -1, axis=0) - emf_x)[:, :-1, 1:-1]
        - (emf_z[:, :-1, 1:] - emf_z[:, :-1, :-1])
    )
    new_bz = padded[7, :, 2:-2, 2:-2] - COURANT_RATIO * (
        emf_y[:, 1:-1, 1:] - emf_y[:, 1:-1, :-1] - (emf_x[:, 1:, 1:-1] - emf_x[:, :-1, 1:-1])
    )
    return jnp.concatenate([hydro, jnp.stack([new_bx, new_by, new_bz])], axis=0)


def shear_correct(strip, sign):
    density = strip[0]
    along = strip[2]
    new_along = along + sign * SHEAR_SPEED * density
    new_energy = strip[4] + sign * SHEAR_SPEED * along + 0.5 * SHEAR_SPEED * SHEAR_SPEED * density
    return jnp.concatenate(
        [strip[0:2], new_along[None], strip[3:4], new_energy[None], strip[5:8]], axis=0
    )


def ghost_remap(strip, offset, own_rows):
    rows = strip.shape[2]
    following = passed_along(strip, "gy", -1)
    joined = jnp.concatenate([strip, following], axis=2)
    blocks = offset // own_rows
    within = offset % own_rows
    for level in range((lax.axis_size("gy") - 1).bit_length()):
        moved = passed_along(joined, "gy", -(1 << level))
        joined = jnp.where((blocks >> level) % 2 == 1, moved, joined)
    return lax.dynamic_slice_in_dim(joined, within, rows, axis=2)


def edge_pad(field, shift, rim):
    own_rows = field.shape[2] - 2 * rim
    widened = with_halo(field, (("gx", 3),), 2)
    lower_ghost = widened[..., :2]
    upper_ghost = widened[..., -2:]
    column = lax.axis_index("gx")
    at_lower = column == 0
    at_upper = column == lax.axis_size("gx") - 1
    strip = jnp.where(at_lower, lower_ghost, upper_ghost)
    total_rows = own_rows * lax.axis_size("gy")
    offset = jnp.where(at_lower, shift, total_rows - shift) % total_rows
    moved = ghost_remap(strip, offset, own_rows)
    fixed = shear_correct(moved, jnp.where(at_lower, 1.0, -1.0).astype(jnp.float32))
    lower_ghost = jnp.where(at_lower, fixed, lower_ghost)
    upper_ghost = jnp.where(at_upper, fixed, upper_ghost)
    return jnp.concatenate([lower_ghost, field, upper_ghost], axis=3)


def on_device(state, offsets):
    current = state
    for section in range(2):
        widened = edge_pad(current, offsets[section], 0)
        current = advance(with_halo(widened, (("gy", 2),), 2))
    return 0.5 * (state + current)


def solution(mesh):
    return jax.shard_map(
        on_device,
        mesh=mesh,
        in_specs=(P(None, None, "gy", "gx"), P()),
        out_specs=P(None, None, "gy", "gx"),
        check_vma=False,
    )
```

profile of v0, /device:TPU:0, one launch (start us, length us, event | category | flops | bytes accessed | tf_op | source)
XLA Modules:
  0.0 99.2 jit_solution(18432387948860057311)
XLA Ops:
  0.0 1.1 %fusion.117 = (f32[8,2,16,2]{3,2,1,0:T(8,128)S(1)}, f32[8,2,16,2]{3,2,1,0:T(8,128)S(1)}) fusion(f32[8,2,16,128]{3,2,1,0:T(8,128)} %param.2), kind=kLoop, calls=%fused_computation.278 | loop fusion | bytes 8192 | tf_op jit(solution)/shard_map/slice | solution.py:27
  1.7 0.9 collective-permute-done
  3.0 6.7 %collective-permute-start.2 = (f32[8,2,16,2]{3,2,1,0:T(8,128)S(1)}, f32[8,2,16,2]{3,2,1,0:T(8,128)S(1)}, u32[]{:S(2)}, u32[]{:S(2)}) collective-permute-start(f32[8,2,16,2]{3,2,1,0:T(8,128)S(1)} %broadcast_select_fusion.5), channel_id=1, source_target_pairs={{1,0},{2,1},{3,2},{4,3},{5,4},{6,5},{7,6},{8,7},{9,8},{10,9},{11,1... | collective-permute-start | bytes 6152 | tf_op jit(solution)/shard_map/ppermute | solution.py:15
  9.9 3.1 %collective-permute-done.2 = f32[8,2,16,2]{3,2,1,0:T(8,128)S(1)} collective-permute-done((f32[8,2,16,2]{3,2,1,0:T(8,128)S(1)}, f32[8,2,16,2]{3,2,1,0:T(8,128)S(1)}, u32[]{:S(2)}, u32[]{:S(2)}) %collective-permute-start.2) | collective-permute-done | bytes 2080 | tf_op jit(solution)/shard_map/ppermute | solution.py:15
  13.2 6.1 %collective-permute-start.3 = (f32[8,2,32,2]{2,0,3,1:T(8,128)S(1)}, f32[8,2,32,2]{2,0,3,1:T(8,128)S(1)}, u32[]{:S(2)}, u32[]{:S(2)}) collective-permute-start(f32[8,2,32,2]{2,0,3,1:T(8,128)S(1)} %pad_maximum_fusion.39), channel_id=1, source_target_pairs={{1,0},{2,1},{3,2},{4,3},{5,4},{6,5},{7,6},{8,7},{9,8},{10,9},{11,1... | collective-permute-start | bytes 12296 | tf_op jit(solution)/shard_map/ppermute | solution.py:15
  21.6 3.5 %collective-permute-done.4 = f32[8,2,32,2]{2,0,3,1:T(8,128)S(1)} collective-permute-done((f32[8,2,32,2]{2,0,3,1:T(8,128)S(1)}, f32[8,2,32,2]{2,0,3,1:T(8,128)S(1)}, u32[]{:S(2)}, u32[]{:S(2)}) %collective-permute-start.4) | collective-permute-done | bytes 4128 | tf_op jit(solution)/shard_map/ppermute | solution.py:15
  25.1 3.7 %collective-permute-done.5 = f32[8,2,32,2]{2,0,3,1:T(8,128)S(1)} collective-permute-done((f32[8,2,32,2]{2,0,3,1:T(8,128)S(1)}, f32[8,2,32,2]{2,0,3,1:T(8,128)S(1)}, u32[]{:S(2)}, u32[]{:S(2)}) %collective-permute-start.5) | collective-permute-done | bytes 4128 | tf_op jit(solution)/shard_map/ppermute | solution.py:15
  28.9 4.6 %collective-permute-done.6 = f32[8,2,32,2]{2,0,3,1:T(8,128)S(1)} collective-permute-done((f32[8,2,32,2]{2,0,3,1:T(8,128)S(1)}, f32[8,2,32,2]{2,0,3,1:T(8,128)S(1)}, u32[]{:S(2)}, u32[]{:S(2)}) %collective-permute-start.6) | collective-permute-done | bytes 4128 | tf_op jit(solution)/shard_map/ppermute | solution.py:15
  35.1 0.9 copy-done
  36.2 3.6 %collective-permute-start.7 = (f32[8,2,2,132]{3,2,1,0:T(2,128)S(1)}, f32[8,2,2,132]{3,2,1,0:T(2,128)S(1)}, u32[]{:S(2)}, u32[]{:S(2)}) collective-permute-start(f32[8,2,2,132]{3,2,1,0:T(2,128)S(1)} %get-tuple-element.61), channel_id=1, source_target_pairs={{0,1},{1,2},{2,3},{3,4},{4,5},{5,6},{6,7},{7,8},{8,9},{9,10},{10,1... | collective-permute-start | bytes 50696 | tf_op jit(solution)/shard_map/ppermute | solution.py:24
  39.8 6.3 %collective-permute-start.8 = (f32[8,2,2,132]{3,2,1,0:T(2,128)S(1)}, f32[8,2,2,132]{3,2,1,0:T(2,128)S(1)}, u32[]{:S(2)}, u32[]{:S(2)}) collective-permute-start(f32[8,2,2,132]{3,2,1,0:T(2,128)S(1)} %get-tuple-element.62), channel_id=1, source_target_pairs={{1,0},{2,1},{3,2},{4,3},{5,4},{6,5},{7,6},{8,7},{9,8},{10,9},{11,1... | collective-permute-start | bytes 50696 | tf_op jit(solution)/shard_map/ppermute | solution.py:27
  46.0 1.8 %collective-permute-done.7 = f32[8,2,2,132]{3,2,1,0:T(2,128)S(1)} collective-permute-done((f32[8,2,2,132]{3,2,1,0:T(2,128)S(1)}, f32[8,2,2,132]{3,2,1,0:T(2,128)S(1)}, u32[]{:S(2)}, u32[]{:S(2)}) %collective-permute-start.7) | collective-permute-done | bytes 16928 | tf_op jit(solution)/shard_map/ppermute | solution.py:24
  51.5 0.8 collective-permute-done.10
  52.5 5.7 %collective-permute-start.11 = (f32[8,2,16,2]{3,2,1,0:T(8,128)S(1)}, f32[8,2,16,2]{3,2,1,0:T(8,128)S(1)}, u32[]{:S(2)}, u32[]{:S(2)}) collective-permute-start(f32[8,2,16,2]{3,2,1,0:T(8,128)S(1)} %broadcast_select_fusion.3), channel_id=1, source_target_pairs={{1,0},{2,1},{3,2},{4,3},{5,4},{6,5},{7,6},{8,7},{9,8},{10,9},{11,1... | collective-permute-start | bytes 6152 | tf_op jit(solution)/shard_map/ppermute | solution.py:15
  58.4 3.1 %collective-permute-done.11 = f32[8,2,16,2]{3,2,1,0:T(8,128)S(1)} collective-permute-done((f32[8,2,16,2]{3,2,1,0:T(8,128)S(1)}, f32[8,2,16,2]{3,2,1,0:T(8,128)S(1)}, u32[]{:S(2)}, u32[]{:S(2)}) %collective-permute-start.11) | collective-permute-done | bytes 2080 | tf_op jit(solution)/shard_map/ppermute | solution.py:15
  61.8 6.1 %collective-permute-start.12 = (f32[8,2,32,2]{2,0,3,1:T(8,128)S(1)}, f32[8,2,32,2]{2,0,3,1:T(8,128)S(1)}, u32[]{:S(2)}, u32[]{:S(2)}) collective-permute-start(f32[8,2,32,2]{2,0,3,1:T(8,128)S(1)} %pad_maximum_fusion.40), channel_id=1, source_target_pairs={{1,0},{2,1},{3,2},{4,3},{5,4},{6,5},{7,6},{8,7},{9,8},{10,9},{11,1... | collective-permute-start | bytes 12296 | tf_op jit(solution)/shard_map/ppermute | solution.py:15
  69.3 0.8 collective-permute-start.13
  70.1 2.9 %collective-permute-done.13 = f32[8,2,32,2]{2,0,3,1:T(8,128)S(1)} collective-permute-done((f32[8,2,32,2]{2,0,3,1:T(8,128)S(1)}, f32[8,2,32,2]{2,0,3,1:T(8,128)S(1)}, u32[]{:S(2)}, u32[]{:S(2)}) %collective-permute-start.13) | collective-permute-done | bytes 4128 | tf_op jit(solution)/shard_map/ppermute | solution.py:15
  73.1 3.7 %collective-permute-done.14 = f32[8,2,32,2]{2,0,3,1:T(8,128)S(1)} collective-permute-done((f32[8,2,32,2]{2,0,3,1:T(8,128)S(1)}, f32[8,2,32,2]{2,0,3,1:T(8,128)S(1)}, u32[]{:S(2)}, u32[]{:S(2)}) %collective-permute-start.14) | collective-permute-done | bytes 4128 | tf_op jit(solution)/shard_map/ppermute | solution.py:15
  76.8 4.6 %collective-permute-done.15 = f32[8,2,32,2]{2,0,3,1:T(8,128)S(1)} collective-permute-done((f32[8,2,32,2]{2,0,3,1:T(8,128)S(1)}, f32[8,2,32,2]{2,0,3,1:T(8,128)S(1)}, u32[]{:S(2)}, u32[]{:S(2)}) %collective-permute-start.15) | collective-permute-done | bytes 4128 | tf_op jit(solution)/shard_map/ppermute | solution.py:15
  82.1 0.7 slice-done
  83.2 4.5 %collective-permute-start.16 = (f32[8,2,2,132]{3,2,1,0:T(2,128)S(1)}, f32[8,2,2,132]{3,2,1,0:T(2,128)S(1)}, u32[]{:S(2)}, u32[]{:S(2)}) collective-permute-start(f32[8,2,2,132]{3,2,1,0:T(2,128)S(1)} %get-tuple-element.42), channel_id=1, source_target_pairs={{0,1},{1,2},{2,3},{3,4},{4,5},{5,6},{6,7},{7,8},{8,9},{9,10},{10,1... | collective-permute-start | bytes 50696 | tf_op jit(solution)/shard_map/ppermute | solution.py:24
  87.7 6.1 %collective-permute-start.17 = (f32[8,2,2,132]{3,2,1,0:T(2,128)S(1)}, f32[8,2,2,132]{3,2,1,0:T(2,128)S(1)}, u32[]{:S(2)}, u32[]{:S(2)}) collective-permute-start(f32[8,2,2,132]{3,2,1,0:T(2,128)S(1)} %get-tuple-element.43), channel_id=1, source_target_pairs={{1,0},{2,1},{3,2},{4,3},{5,4},{6,5},{7,6},{8,7},{9,8},{10,9},{11,1... | collective-permute-start | bytes 50696 | tf_op jit(solution)/shard_map/ppermute | solution.py:27
  93.8 1.8 %collective-permute-done.16 = f32[8,2,2,132]{3,2,1,0:T(2,128)S(1)} collective-permute-done((f32[8,2,2,132]{3,2,1,0:T(2,128)S(1)}, f32[8,2,2,132]{3,2,1,0:T(2,128)S(1)}, u32[]{:S(2)}, u32[]{:S(2)}) %collective-permute-start.16) | collective-permute-done | bytes 16928 | tf_op jit(solution)/shard_map/ppermute | solution.py:24
  (124 shorter events, 12.7 us)
Async XLA Ops:
  1.1 1.5 %collective-permute-start = (f32[8,2,16,2]{3,2,1,0:T(8,128)S(1)}, f32[8,2,16,2]{3,2,1,0:T(8,128)S(1)}, u32[]{:S(2)}, u32[]{:S(2)}) collective-permute-start(f32[8,2,16,2]{3,2,1,0:T(8,128)S(1)} %get-tuple-element.85), channel_id=1, source_target_pairs={{0,16},{16,0},{1,17},{17,1},{2,18},{18,2},{3,19},{19,3},{4,20},{20... | collective-permute-start | bytes 6152 | tf_op jit(solution)/shard_map/ppermute | solution.py:24
  1.6 1.3 %collective-permute-start.1 = (f32[8,2,16,2]{3,2,1,0:T(8,128)S(1)}, f32[8,2,16,2]{3,2,1,0:T(8,128)S(1)}, u32[]{:S(2)}, u32[]{:S(2)}) collective-permute-start(f32[8,2,16,2]{3,2,1,0:T(8,128)S(1)} %get-tuple-element.84), channel_id=1, source_target_pairs={{16,0},{0,16},{17,1},{1,17},{18,2},{2,18},{19,3},{3,19},{20,4},{4,... | collective-permute-start | bytes 6152 | tf_op jit(solution)/shard_map/ppermute | solution.py:27
  3.0 10.0 %collective-permute-start.2 = (f32[8,2,16,2]{3,2,1,0:T(8,128)S(1)}, f32[8,2,16,2]{3,2,1,0:T(8,128)S(1)}, u32[]{:S(2)}, u32[]{:S(2)}) collective-permute-start(f32[8,2,16,2]{3,2,1,0:T(8,128)S(1)} %broadcast_select_fusion.5), channel_id=1, source_target_pairs={{1,0},{2,1},{3,2},{4,3},{5,4},{6,5},{7,6},{8,7},{9,8},{10,9},{11,1... | collective-permute-start | bytes 6152 | tf_op jit(solution)/shard_map/ppermute | solution.py:15
  13.1 6.2 %copy-start.3 = (s32[2]{0:T(128)S(1)}, s32[2]{0:T(128)}, u32[]{:S(2)}) copy-start(s32[2]{0:T(128)} %param.3) | copy-start | bytes 28
  13.2 8.1 %collective-permute-start.3 = (f32[8,2,32,2]{2,0,3,1:T(8,128)S(1)}, f32[8,2,32,2]{2,0,3,1:T(8,128)S(1)}, u32[]{:S(2)}, u32[]{:S(2)}) collective-permute-start(f32[8,2,32,2]{2,0,3,1:T(8,128)S(1)} %pad_maximum_fusion.39), channel_id=1, source_target_pairs={{1,0},{2,1},{3,2},{4,3},{5,4},{6,5},{7,6},{8,7},{9,8},{10,9},{11,1... | collective-permute-start | bytes 12296 | tf_op jit(solution)/shard_map/ppermute | solution.py:15
  21.3 3.8 %collective-permute-start.4 = (f32[8,2,32,2]{2,0,3,1:T(8,128)S(1)}, f32[8,2,32,2]{2,0,3,1:T(8,128)S(1)}, u32[]{:S(2)}, u32[]{:S(2)}) collective-permute-start(f32[8,2,32,2]{2,0,3,1:T(8,128)S(1)} %broadcast_select_fusion.9), channel_id=1, source_target_pairs={{2,0},{3,1},{4,2},{5,3},{6,4},{7,5},{8,6},{9,7},{10,8},{11,9},{12,... | collective-permute-start | bytes 12296 | tf_op jit(solution)/shard_map/ppermute | solution.py:15
  25.1 3.7 %collective-permute-start.5 = (f32[8,2,32,2]{2,0,3,1:T(8,128)S(1)}, f32[8,2,32,2]{2,0,3,1:T(8,128)S(1)}, u32[]{:S(2)}, u32[]{:S(2)}) collective-permute-start(f32[8,2,32,2]{2,0,3,1:T(8,128)S(1)} %broadcast_select_fusion.10), channel_id=1, source_target_pairs={{4,0},{5,1},{6,2},{7,3},{8,4},{9,5},{10,6},{11,7},{12,8},{13,9},{1... | collective-permute-start | bytes 12296 | tf_op jit(solution)/shard_map/ppermute | solution.py:15
  28.9 4.6 %collective-permute-start.6 = (f32[8,2,32,2]{2,0,3,1:T(8,128)S(1)}, f32[8,2,32,2]{2,0,3,1:T(8,128)S(1)}, u32[]{:S(2)}, u32[]{:S(2)}) collective-permute-start(f32[8,2,32,2]{2,0,3,1:T(8,128)S(1)} %broadcast_select_fusion.11), channel_id=1, source_target_pairs={{8,0},{9,1},{10,2},{11,3},{12,4},{13,5},{14,6},{15,7},{0,8},{1,9},... | collective-permute-start | bytes 12296 | tf_op jit(solution)/shard_map/ppermute | solution.py:15
  33.6 0.6 copy-start.2
  34.2 0.7 slice-start.1
  35.1 0.9 copy-start
  36.2 11.7 %collective-permute-start.7 = (f32[8,2,2,132]{3,2,1,0:T(2,128)S(1)}, f32[8,2,2,132]{3,2,1,0:T(2,128)S(1)}, u32[]{:S(2)}, u32[]{:S(2)}) collective-permute-start(f32[8,2,2,132]{3,2,1,0:T(2,128)S(1)} %get-tuple-element.61), channel_id=1, source_target_pairs={{0,1},{1,2},{2,3},{3,4},{4,5},{5,6},{6,7},{7,8},{8,9},{9,10},{10,1... | collective-permute-start | bytes 50696 | tf_op jit(solution)/shard_map/ppermute | solution.py:24
  39.8 8.1 %collective-permute-start.8 = (f32[8,2,2,132]{3,2,1,0:T(2,128)S(1)}, f32[8,2,2,132]{3,2,1,0:T(2,128)S(1)}, u32[]{:S(2)}, u32[]{:S(2)}) collective-permute-start(f32[8,2,2,132]{3,2,1,0:T(2,128)S(1)} %get-tuple-element.62), channel_id=1, source_target_pairs={{1,0},{2,1},{3,2},{4,3},{5,4},{6,5},{7,6},{8,7},{9,8},{10,9},{11,1... | collective-permute-start | bytes 50696 | tf_op jit(solution)/shard_map/ppermute | solution.py:27
  50.9 1.4 %collective-permute-start.10 = (f32[8,2,16,2]{3,2,1,0:T(8,128)S(1)}, f32[8,2,16,2]{3,2,1,0:T(8,128)S(1)}, u32[]{:S(2)}, u32[]{:S(2)}) collective-permute-start(f32[8,2,16,2]{3,2,1,0:T(8,128)S(1)} %get-tuple-element.80), channel_id=1, source_target_pairs={{16,0},{0,16},{17,1},{1,17},{18,2},{2,18},{19,3},{3,19},{20,4},{4,... | collective-permute-start | bytes 6152 | tf_op jit(solution)/shard_map/ppermute | solution.py:27
  51.0 1.5 %collective-permute-start.9 = (f32[8,2,16,2]{3,2,1,0:T(8,128)S(1)}, f32[8,2,16,2]{3,2,1,0:T(8,128)S(1)}, u32[]{:S(2)}, u32[]{:S(2)}) collective-permute-start(f32[8,2,16,2]{3,2,1,0:T(8,128)S(1)} %get-tuple-element.81), channel_id=1, source_target_pairs={{0,16},{16,0},{1,17},{17,1},{2,18},{18,2},{3,19},{19,3},{4,20},{20... | collective-permute-start | bytes 6152 | tf_op jit(solution)/shard_map/ppermute | solution.py:24
  52.5 9.0 %collective-permute-start.11 = (f32[8,2,16,2]{3,2,1,0:T(8,128)S(1)}, f32[8,2,16,2]{3,2,1,0:T(8,128)S(1)}, u32[]{:S(2)}, u32[]{:S(2)}) collective-permute-start(f32[8,2,16,2]{3,2,1,0:T(8,128)S(1)} %broadcast_select_fusion.3), channel_id=1, source_target_pairs={{1,0},{2,1},{3,2},{4,3},{5,4},{6,5},{7,6},{8,7},{9,8},{10,9},{11,1... | collective-permute-start | bytes 6152 | tf_op jit(solution)/shard_map/ppermute | solution.py:15
  61.8 7.5 %collective-permute-start.12 = (f32[8,2,32,2]{2,0,3,1:T(8,128)S(1)}, f32[8,2,32,2]{2,0,3,1:T(8,128)S(1)}, u32[]{:S(2)}, u32[]{:S(2)}) collective-permute-start(f32[8,2,32,2]{2,0,3,1:T(8,128)S(1)} %pad_maximum_fusion.40), channel_id=1, source_target_pairs={{1,0},{2,1},{3,2},{4,3},{5,4},{6,5},{7,6},{8,7},{9,8},{10,9},{11,1... | collective-permute-start | bytes 12296 | tf_op jit(solution)/shard_map/ppermute | solution.py:15
  69.3 3.7 %collective-permute-start.13 = (f32[8,2,32,2]{2,0,3,1:T(8,128)S(1)}, f32[8,2,32,2]{2,0,3,1:T(8,128)S(1)}, u32[]{:S(2)}, u32[]{:S(2)}) collective-permute-start(f32[8,2,32,2]{2,0,3,1:T(8,128)S(1)} %broadcast_select_fusion.6), channel_id=1, source_target_pairs={{2,0},{3,1},{4,2},{5,3},{6,4},{7,5},{8,6},{9,7},{10,8},{11,9},{12,... | collective-permute-start | bytes 12296 | tf_op jit(solution)/shard_map/ppermute | solution.py:15
  73.0 3.7 %collective-permute-start.14 = (f32[8,2,32,2]{2,0,3,1:T(8,128)S(1)}, f32[8,2,32,2]{2,0,3,1:T(8,128)S(1)}, u32[]{:S(2)}, u32[]{:S(2)}) collective-permute-start(f32[8,2,32,2]{2,0,3,1:T(8,128)S(1)} %broadcast_select_fusion.7), channel_id=1, source_target_pairs={{4,0},{5,1},{6,2},{7,3},{8,4},{9,5},{10,6},{11,7},{12,8},{13,9},{1... | collective-permute-start | bytes 12296 | tf_op jit(solution)/shard_map/ppermute | solution.py:15
  76.8 4.6 %collective-permute-start.15 = (f32[8,2,32,2]{2,0,3,1:T(8,128)S(1)}, f32[8,2,32,2]{2,0,3,1:T(8,128)S(1)}, u32[]{:S(2)}, u32[]{:S(2)}) collective-permute-start(f32[8,2,32,2]{2,0,3,1:T(8,128)S(1)} %broadcast_select_fusion.8), channel_id=1, source_target_pairs={{8,0},{9,1},{10,2},{11,3},{12,4},{13,5},{14,6},{15,7},{0,8},{1,9},... | collective-permute-start | bytes 12296 | tf_op jit(solution)/shard_map/ppermute | solution.py:15
  81.5 0.6 copy-start.1
  82.1 0.7 slice-start
  83.2 12.4 %collective-permute-start.16 = (f32[8,2,2,132]{3,2,1,0:T(2,128)S(1)}, f32[8,2,2,132]{3,2,1,0:T(2,128)S(1)}, u32[]{:S(2)}, u32[]{:S(2)}) collective-permute-start(f32[8,2,2,132]{3,2,1,0:T(2,128)S(1)} %get-tuple-element.42), channel_id=1, source_target_pairs={{0,1},{1,2},{2,3},{3,4},{4,5},{5,6},{6,7},{7,8},{8,9},{9,10},{10,1... | collective-permute-start | bytes 50696 | tf_op jit(solution)/shard_map/ppermute | solution.py:24
  87.7 8.0 %collective-permute-start.17 = (f32[8,2,2,132]{3,2,1,0:T(2,128)S(1)}, f32[8,2,2,132]{3,2,1,0:T(2,128)S(1)}, u32[]{:S(2)}, u32[]{:S(2)}) collective-permute-start(f32[8,2,2,132]{3,2,1,0:T(2,128)S(1)} %get-tuple-element.43), channel_id=1, source_target_pairs={{1,0},{2,1},{3,2},{4,3},{5,4},{6,5},{7,6},{8,7},{9,8},{10,9},{11,1... | collective-permute-start | bytes 50696 | tf_op jit(solution)/shard_map/ppermute | solution.py:27
where the time goes:
time: 99.4 us; the launch traced here: 99.2 us
  starting transfers between devices  47.4 us (48%)
  waiting for transfers between devices  35.3 us (36%)
  local copies, waits for them, and re-layouts  6.75 us (7%)
  other arithmetic  6.41 us (6%)
  between operations  3.35 us (3%)
    ppermute x10, waiting for transfers between devices, passed_along(): return lax.ppermute(block, axis, route)  29.3 us
    ppermute x10, starting transfers between devices, passed_along(): return lax.ppermute(block, axis, route)  25.7 us
    ppermute x4, starting transfers between devices, with_halo(): lax.ppermute(lax.slice_in_dim(block, 0, width, axis=dim), axis, backward)  12.5 us
    ppermute x4, starting transfers between devices, with_halo(): lax.ppermute(lax.slice_in_dim(block, block.shape[dim] - width, None, axis...  9.13 us
    ppermute x4, waiting for transfers between devices, with_halo(): lax.ppermute(lax.slice_in_dim(block, block.shape[dim] - width, None, axis...  4.75 us
    unnamed x8, local copies, waits for them, and re-layouts  2.05 us
  transfers between devices with their start and end apart: 18, of which 15 were waited for; matrix products, arithmetic and copies ran while one was open for 1% of the time, Pallas kernels for 0%

commit v1 on v0

v1 whole, which is shorter than its diff:
```python
import functools

import jax
import jax.numpy as jnp
from jax import lax
from jax.experimental import pallas as pl
from jax.experimental.pallas import tpu as pltpu
from jax.sharding import PartitionSpec as P

ADIABATIC = 5.0 / 3.0
SIGNAL_SPEED = 4.0
COURANT_RATIO = 0.06
SHEAR_SPEED = 1.5
MESH = pl.DeviceIdType.MESH


def turned(value, shift, axis):
    return pltpu.roll(value, shift % value.shape[axis], axis)


def advance(fields, depth):
    xm = lambda a: turned(a, 1, 1)
    xp = lambda a: turned(a, -1, 1)
    ym = lambda a: turned(a, 1, 0)
    yp = lambda a: turned(a, -1, 0)
    half_a = 0.5 * SIGNAL_SPEED
    levels = range(depth)
    below = lambda z: (z - 1) % depth
    above = lambda z: (z + 1) % depth

    cells, flux_z, emf = [], [], []
    for z in levels:
        rho, mx, my, mz, en, bx, by, bz = (fields[f][z] for f in range(8))
        cx = 0.5 * (bx + xp(bx))
        cy = 0.5 * (by + yp(by))
        cz = 0.5 * (bz + fields[7][above(z)])
        inv = 1.0 / rho
        vx, vy, vz = mx * inv, my * inv, mz * inv
        bsq = cx * cx + cy * cy + cz * cz
        pressure = (ADIABATIC - 1.0) * (en - 0.5 * (mx * vx + my * vy + mz * vz) - 0.5 * bsq)
        pt = pressure + 0.5 * bsq
        vb = vx * cx + vy * cy + vz * cz
        ept = en + pt
        mxy = mx * vy - cx * cy
        mxz = mx * vz - cx * cz
        myz = my * vz - cy * cz
        flux_x = (mx, mx * vx - cx * cx + pt, mxy, mxz, ept * vx - cx * vb)
        flux_y = (my, mxy, my * vy - cy * cy + pt, myz, ept * vy - cy * vb)
        flux_v = (mz, mxz, myz, mz * vz - cz * cz + pt, ept * vz - cz * vb)
        q = (rho, mx, my, mz, en)
        total = []
        ups, downs = [], []
        for f in range(5):
            aq = half_a * q[f]
            hx, hy, hz = 0.5 * flux_x[f], 0.5 * flux_y[f], 0.5 * flux_v[f]
            face_x = xm(hx + aq) + (hx - aq)
            face_y = ym(hy + aq) + (hy - aq)
            total.append((xp(face_x) - face_x) + (yp(face_y) - face_y))
            ups.append(hz + aq)
            downs.append(hz - aq)
        gz = 0.5 * (vx * cy - vy * cx)
        gx = 0.5 * (vy * cz - vz * cy)
        gy = 0.5 * (vx * cz - vz * cx)
        ax, ay, az = half_a * cx, half_a * cy, half_a * cz
        fx_by = xm(gz + ay) + (gz - ay)
        fy_bx = ym(ax - gz) - (gz + ax)
        ez = 0.25 * ((fy_bx + xm(fy_bx)) - (fx_by + ym(fx_by)))
        fy_bz = ym(gx + az) + (gx - az)
        fx_bz = xm(gy + az) + (gy - az)
        cells.append((q, total, ups, downs))
        emf.append((ez, fy_bz, fx_bz, ay - gx, gx + ay, ax - gy, gy + ax))

    ex, ey = [], []
    for z in levels:
        fz_by = emf[below(z)][3] - emf[z][4]
        fz_bx = emf[below(z)][5] - emf[z][6]
        ex.append(0.25 * ((fz_by + ym(fz_by)) - (emf[z][1] + emf[below(z)][1])))
        ey.append(0.25 * ((emf[z][2] + emf[below(z)][2]) - (fz_bx + xm(fz_bx))))

    face_z = [
        [cells[below(z)][2][f] + cells[z][3][f] for f in range(5)] for z in levels
    ]
    out = [[None] * depth for _ in range(8)]
    for z in levels:
        q, total, _, _ = cells[z]
        for f in range(5):
            change = total[f] + (face_z[above(z)][f] - face_z[z][f])
            out[f][z] = q[f] - COURANT_RATIO * change
        ez = emf[z][0]
        dz_ey = ey[above(z)] - ey[z]
        dz_ex = ex[above(z)] - ex[z]
        out[5][z] = fields[5][z] - COURANT_RATIO * ((yp(ez) - ez) - dz_ey)
        out[6][z] = fields[6][z] - COURANT_RATIO * (dz_ex - (xp(ez) - ez))
        out[7][z] = fields[7][z] - COURANT_RATIO * ((xp(ey[z]) - ey[z]) - (yp(ex[z]) - ex[z]))
    return out


def kernel(
    nx, ny, offsets_ref, state_ref, out_ref, pack, rim_low, rim_high, own, left, right,
    send_own, recv_own, send_left, recv_left, send_right, recv_right, send_rim, recv_rim,
):
    depth, rows, lanes = state_ref.shape[1:]
    two = nx == 2
    cx, cy = lax.axis_index("gx"), lax.axis_index("gy")
    lx, rx = lax.rem(cx + nx - 1, nx), lax.rem(cx + 1, nx)
    up, down = lax.rem(cy + 1, ny), lax.rem(cy + ny - 1, ny)
    others = [rx] if two else [lx, rx]

    barrier = pltpu.get_barrier_semaphore()

    def greet(d, _):
        there = lax.rem(cy + d, ny)

        @pl.when(d > 0)
        def _():
            pl.semaphore_signal(barrier, inc=1, device_id=(cx, there), device_id_type=MESH)

        for column in others:
            pl.semaphore_signal(barrier, inc=1, device_id=(column, there), device_id_type=MESH)
        return 0

    lax.fori_loop(0, ny, greet, 0)

    lane = lax.broadcasted_iota(jnp.int32, (8, lanes), 1)
    sub = lane % 8
    part = lane // 8
    sublane = lax.broadcasted_iota(jnp.int32, (8, lanes), 0)
    mine = pl.multiple_of(cy * rows, rows)
    for t in range(0, rows, 8):
        packed = jnp.zeros((8, lanes), jnp.float32)
        for f in range(8):
            for z in range(depth):
                k = f * depth + z
                moved = turned(state_ref[f, z, t : t + 8, :], 8 * k + 4, 1)
                packed = jnp.where(part == k, moved, packed)
        pack[t : t + 8, :] = packed
        own[pl.ds(pl.multiple_of(mine + t, 8), 8), :] = packed

    pl.semaphore_wait(barrier, ny * (1 + len(others)) - 1)

    rims = [
        pltpu.make_async_remote_copy(
            src_ref=state_ref.at[:, :, pl.ds(rows - 8, 8), :], dst_ref=rim_low,
            send_sem=send_rim.at[0], recv_sem=recv_rim.at[0],
            device_id=(cx, up), device_id_type=MESH,
        ),
        pltpu.make_async_remote_copy(
            src_ref=state_ref.at[:, :, pl.ds(0, 8), :], dst_ref=rim_high,
            send_sem=send_rim.at[1], recv_sem=recv_rim.at[1],
            device_id=(cx, down), device_id_type=MESH,
        ),
    ]

    lines = [(own, cx, send_own, recv_own)]
    if two:
        lines.append((left, rx, send_left, recv_left))
    else:
        lines.append((left, rx, send_left, recv_left))
        lines.append((right, lx, send_right, recv_right))

    def strip_copy(line, target, source):
        buffer, column, send, recv = line
        return pltpu.make_async_remote_copy(
            src_ref=pack,
            dst_ref=buffer.at[pl.ds(pl.multiple_of(source * rows, rows), rows), :],
            send_sem=send.at[target], recv_sem=recv.at[source],
            device_id=(column, target), device_id_type=MESH,
        )

    def each(action):
        def step(d, _):
            there = lax.rem(cy + d, ny)

            @pl.when(d > 0)
            def _():
                action(lines[0], there)

            for line in lines[1:]:
                action(line, there)
            return 0

        lax.fori_loop(0, ny, step, 0)

    each(lambda line, there: strip_copy(line, there, cy).start())
    for copy in rims:
        copy.start()

    each(lambda line, there: strip_copy(line, there, there).wait_recv())
    for copy in rims:
        copy.wait_recv()

    total_rows = rows * ny
    for buffer, *_ in lines:
        buffer[total_rows : total_rows + 8, :] = buffer[0:8, :]
    left_buf = left
    right_buf = left if two else right

    at_lower = cx == 0
    at_upper = cx == nx - 1
    lower_i = at_lower.astype(jnp.int32)
    upper_i = at_upper.astype(jnp.int32)
    lower_f = at_lower.astype(jnp.float32)
    upper_f = at_upper.astype(jnp.float32)
    first, second = offsets_ref[0], offsets_ref[1]
    base = cy * rows

    def slab(buffer, shift):
        def part_at(j):
            return buffer[pl.ds(lax.rem(base + shift + (j + 2 * total_rows), total_rows), 8), :]

        edge = jnp.where(sublane < 4, part_at(rows), part_at(-8))
        return [part_at(t) for t in range(0, rows, 8)] + [edge]

    field_of = part // depth
    def corrected(tiles, sign):
        along = jnp.where((field_of == 2) | (field_of == 4), sign * SHEAR_SPEED, 0.0)
        square = jnp.where(field_of == 4, sign * sign * (0.5 * SHEAR_SPEED * SHEAR_SPEED), 0.0)
        return [
            p + along * turned(p, 16 * depth, 1) + square * turned(p, 32 * depth, 1) for p in tiles
        ]

    ghost_l = corrected(slab(left_buf, lower_i * first), lower_f)
    ghost_r = corrected(slab(right_buf, -upper_i * first), -upper_f)
    side = lower_i - upper_i
    side_f = lower_f - upper_f
    far = slab(left_buf, side * second)
    if not two:
        far_r = slab(right_buf, side * second)
        far = [jnp.where(at_upper, b, a) for a, b in zip(far, far_r)]
    near = corrected(slab(own, side * (second - first)), -side_f)

    ghosts = [
        jnp.where(sub < 4, turned(b, -4, 1), turned(a, 4, 1)) for a, b in zip(ghost_l, ghost_r)
    ]
    from_far = (sub < 4) == at_lower
    joint = [jnp.where(from_far, a, b) for a, b in zip(far, near)]

    stack = lambda tiles: jnp.concatenate(tiles, axis=0)
    ghosts, joint = stack(ghosts), stack(joint)
    height = rows + 8
    wide = lax.broadcasted_iota(jnp.int32, (height, lanes), 1)
    main, strip = [], []
    for f in range(8):
        main.append([])
        strip.append([])
        for z in range(depth):
            k = f * depth + z
            edge = jnp.where(sublane < 4, rim_high[f, z], rim_low[f, z])
            m = jnp.concatenate([state_ref[f, z], edge], axis=0)
            s = jnp.where(wide < 40, turned(m, 8, 1), m)
            s = jnp.where(wide < 8, turned(ghosts, -8 * k, 1), s)
            s = jnp.where((wide >= 40) & (wide < 48), turned(joint, 40 - 8 * k, 1), s)
            main[f].append(m)
            strip[f].append(s)

    main = advance(main, depth)
    strip = advance(strip, depth)
    back = jnp.where(at_lower, lanes - 36, lanes - 44)
    takes = ((wide == 7) & at_lower) | ((wide < 2) & at_upper)
    for z in range(depth):
        moved = [pltpu.roll(strip[f][z], back, 1) for f in range(8)]
        rho, my = moved[0], moved[2]
        moved[2] = my + (side_f * SHEAR_SPEED) * rho
        moved[4] = moved[4] + (side_f * SHEAR_SPEED) * my + (0.5 * SHEAR_SPEED * SHEAR_SPEED) * rho
        for f in range(8):
            strip[f][z] = jnp.where(takes, moved[f], strip[f][z])
    main = advance(main, depth)
    strip = advance(strip, depth)

    inner = wide[:rows]
    for f in range(8):
        for z in range(depth):
            s = strip[f][z][:rows]
            new = jnp.where(inner < 4, turned(s, -8, 1), jnp.where(inner >= lanes - 8, s, main[f][z][:rows]))
            out_ref[f, z] = 0.5 * (state_ref[f, z] + new)

    each(lambda line, there: strip_copy(line, there, cy).wait_send())
    for copy in rims:
        copy.wait_send()


def on_device(nx, ny, state, offsets):
    fields, depth, rows, lanes = state.shape
    dma = pltpu.SemaphoreType.DMA
    gathered = pltpu.VMEM((rows * ny + 8, lanes), jnp.float32)
    spare = gathered if nx > 2 else pltpu.VMEM((8, lanes), jnp.float32)
    return pl.pallas_call(
        functools.partial(kernel, nx, ny),
        out_shape=jax.ShapeDtypeStruct(state.shape, state.dtype),
        in_specs=[
            pl.BlockSpec(memory_space=pltpu.SMEM),
            pl.BlockSpec(memory_space=pltpu.VMEM),
        ],
        out_specs=pl.BlockSpec(memory_space=pltpu.VMEM),
        scratch_shapes=[
            pltpu.VMEM((rows, lanes), jnp.float32),
            pltpu.VMEM((fields, depth, 8, lanes), jnp.float32),
            pltpu.VMEM((fields, depth, 8, lanes), jnp.float32),
            gathered, gathered, spare,
            dma((ny,)), dma((ny,)), dma((ny,)), dma((ny,)), dma((ny,)), dma((ny,)),
            dma((2,)), dma((2,)),
        ],
        compiler_params=pltpu.CompilerParams(collective_id=0, has_side_effects=True),
    )(offsets, state)


def solution(mesh):
    nx, ny = mesh.shape["gx"], mesh.shape["gy"]
    return jax.shard_map(
        functools.partial(on_device, nx, ny),
        mesh=mesh,
        in_specs=(P(None, None, "gy", "gx"), P()),
        out_specs=P(None, None, "gy", "gx"),
        check_vma=False,
    )
```

time: 99.4 us -> 21 us (0.21)
  starting transfers between devices: 47.4 us -> 0 us
  waiting for transfers between devices: 35.3 us -> 0 us
  Pallas kernels: 0 us -> 19.3 us
  other arithmetic: 6.41 us -> 0 us
  local copies, waits for them, and re-layouts: 6.75 us -> 1.57 us
  between operations: 3.35 us -> 0.01 us
    ppermute x18 -> x0, starting transfers between devices: 47.4 us -> none  [the longest x10 25.7 us: passed_along(): return lax.ppermute(block, axis, route)]
    ppermute x18 -> x0, waiting for transfers between devices: 35.3 us -> none  [the longest x10 29.3 us: passed_along(): return lax.ppermute(block, axis, route)]
    pallas_call x0 -> x1, Pallas kernels: none -> 19.3 us  [on_device(): pl.pallas_call(functools.partial(kernel, nx, ny), out_shape=jax.ShapeDtyp...]
    slice x27 -> x0, local copies, waits for them, and re-layouts: 3.68 us -> none  [the longest x4 1.37 us: shear_correct(): strip[0:2]]
    sub x13 -> x0, other arithmetic: 1.81 us -> none  [the longest x2 0.54 us: advance(): 0.5 * (flux_phys[..., :-1] + flux_phys[..., 1:])]
    mul x9 -> x0, other arithmetic: 1.25 us -> none  [the longest x1 0.68 us: on_device(): return 0.5 * (state + current)]
    unnamed x8 -> x1, local copies, waits for them, and re-layouts: 2.05 us -> 1.57 us
  transfers between devices with their start and end apart: 18 -> 0, of which waited for: 15 -> 0; matrix products, arithmetic and copies ran while one was open for 1% -> 0% of each run, Pallas kernels for 0% -> 0%
where the time goes in v1:
time: 21 us; the launch traced here: 20.9 us
  Pallas kernels  19.3 us (92%)
  local copies, waits for them, and re-layouts  1.57 us (7%)
    pallas_call x1, Pallas kernels, on_device(): pl.pallas_call(functools.partial(kernel, nx, ny), out_shape=jax.ShapeDtyp...  19.3 us
    unnamed x1, local copies, waits for them, and re-layouts  1.57 us

profile of v1, /device:TPU:0, one launch (start us, length us, event | category | flops | bytes accessed | tf_op | source)
XLA Modules:
  0.0 20.9 jit_solution(15856674258715131530)
XLA Ops:
  0.0 19.3 %shard_map.28 = f32[8,2,16,128]{3,2,1,0:T(8,128)} custom-call(s32[2]{0:T(128)} %offsets_ref.1, f32[8,2,16,128]{3,2,1,0:T(8,128)} %state_ref.1), custom_call_target="tpu_custom_call" | custom-call | tf_op jit(solution)/shard_map/pallas_call | solution.py:287
  19.3 1.6 %copy.4 = f32[8,2,16,128]{3,2,1,0:T(8,128)} copy(f32[8,2,16,128]{3,2,1,0:T(8,128)} %shard_map.28) | data formatting | bytes 262144

commit v2 on v1

v2 whole, which is shorter than its diff:
```python
import functools

import jax
import jax.numpy as jnp
from jax import lax
from jax.experimental import pallas as pl
from jax.experimental.pallas import tpu as pltpu
from jax.sharding import PartitionSpec as P

ADIABATIC = 5.0 / 3.0
SIGNAL_SPEED = 4.0
COURANT_RATIO = 0.06
SHEAR_SPEED = 1.5
MESH = pl.DeviceIdType.MESH


def turned(value, shift, axis):
    return pltpu.roll(value, shift % value.shape[axis], axis)


def advance(fields, depth):
    xm = lambda a: turned(a, 1, 1)
    xp = lambda a: turned(a, -1, 1)
    ym = lambda a: turned(a, 1, 0)
    yp = lambda a: turned(a, -1, 0)
    half_a = 0.5 * SIGNAL_SPEED
    levels = range(depth)
    below = lambda z: (z - 1) % depth
    above = lambda z: (z + 1) % depth

    cells, flux_z, emf = [], [], []
    for z in levels:
        rho, mx, my, mz, en, bx, by, bz = (fields[f][z] for f in range(8))
        cx = 0.5 * (bx + xp(bx))
        cy = 0.5 * (by + yp(by))
        cz = 0.5 * (bz + fields[7][above(z)])
        inv = 1.0 / rho
        vx, vy, vz = mx * inv, my * inv, mz * inv
        bsq = cx * cx + cy * cy + cz * cz
        pressure = (ADIABATIC - 1.0) * (en - 0.5 * (mx * vx + my * vy + mz * vz) - 0.5 * bsq)
        pt = pressure + 0.5 * bsq
        vb = vx * cx + vy * cy + vz * cz
        ept = en + pt
        mxy = mx * vy - cx * cy
        mxz = mx * vz - cx * cz
        myz = my * vz - cy * cz
        flux_x = (mx, mx * vx - cx * cx + pt, mxy, mxz, ept * vx - cx * vb)
        flux_y = (my, mxy, my * vy - cy * cy + pt, myz, ept * vy - cy * vb)
        flux_v = (mz, mxz, myz, mz * vz - cz * cz + pt, ept * vz - cz * vb)
        q = (rho, mx, my, mz, en)
        total = []
        ups, downs = [], []
        for f in range(5):
            aq = half_a * q[f]
            hx, hy, hz = 0.5 * flux_x[f], 0.5 * flux_y[f], 0.5 * flux_v[f]
            face_x = xm(hx + aq) + (hx - aq)
            face_y = ym(hy + aq) + (hy - aq)
            total.append((xp(face_x) - face_x) + (yp(face_y) - face_y))
            ups.append(hz + aq)
            downs.append(hz - aq)
        gz = 0.5 * (vx * cy - vy * cx)
        gx = 0.5 * (vy * cz - vz * cy)
        gy = 0.5 * (vx * cz - vz * cx)
        ax, ay, az = half_a * cx, half_a * cy, half_a * cz
        fx_by = xm(gz + ay) + (gz - ay)
        fy_bx = ym(ax - gz) - (gz + ax)
        ez = 0.25 * ((fy_bx + xm(fy_bx)) - (fx_by + ym(fx_by)))
        fy_bz = ym(gx + az) + (gx - az)
        fx_bz = xm(gy + az) + (gy - az)
        cells.append((q, total, ups, downs))
        emf.append((ez, fy_bz, fx_bz, ay - gx, gx + ay, ax - gy, gy + ax))

    ex, ey = [], []
    for z in levels:
        fz_by = emf[below(z)][3] - emf[z][4]
        fz_bx = emf[below(z)][5] - emf[z][6]
        ex.append(0.25 * ((fz_by + ym(fz_by)) - (emf[z][1] + emf[below(z)][1])))
        ey.append(0.25 * ((emf[z][2] + emf[below(z)][2]) - (fz_bx + xm(fz_bx))))

    face_z = [
        [cells[below(z)][2][f] + cells[z][3][f] for f in range(5)] for z in levels
    ]
    out = [[None] * depth for _ in range(8)]
    for z in levels:
        q, total, _, _ = cells[z]
        for f in range(5):
            change = total[f] + (face_z[above(z)][f] - face_z[z][f])
            out[f][z] = q[f] - COURANT_RATIO * change
        ez = emf[z][0]
        dz_ey = ey[above(z)] - ey[z]
        dz_ex = ex[above(z)] - ex[z]
        out[5][z] = fields[5][z] - COURANT_RATIO * ((yp(ez) - ez) - dz_ey)
        out[6][z] = fields[6][z] - COURANT_RATIO * (dz_ex - (xp(ez) - ez))
        out[7][z] = fields[7][z] - COURANT_RATIO * ((xp(ey[z]) - ey[z]) - (yp(ex[z]) - ex[z]))
    return out


def kernel(
    nx, ny, offsets_ref, input_ref, out_ref, state_ref, packs, rim_up, rim_down, rim_low, rim_high,
    gather_low, gather_high, halo_left, halo_right, joined,
    send_edge, recv_edge, send_side, recv_side, send_rim, recv_rim, load_sem,
):
    fields, depth, rows, lanes = state_ref.shape
    cx, cy = lax.axis_index("gx"), lax.axis_index("gy")
    up, down = lax.rem(cy + 1, ny), lax.rem(cy + ny - 1, ny)
    at_lower = cx == 0
    at_upper = cx == nx - 1
    at_edge = at_lower | at_upper
    lower_i = at_lower.astype(jnp.int32)
    upper_i = at_upper.astype(jnp.int32)
    lower_f = at_lower.astype(jnp.float32)
    upper_f = at_upper.astype(jnp.float32)
    opposite = jnp.where(at_lower, nx - 1, 0)
    near_rows = (down, cy, up)

    def around(action):
        def step(d, _):
            there = lax.rem(cy + d, ny)
            action(opposite, there)

            @pl.when(d < ny)
            def _():
                action(cx, there)

            return 0

        if ny > 16:
            lax.fori_loop(1, ny + 1, step, 0)
            return
        for d in range(1, ny + 1):
            there = lax.rem(cy + d, ny)
            action(opposite, there)
            if d < ny:
                action(cx, there)

    barrier = pltpu.get_barrier_semaphore()

    def greet(column, row):
        pl.semaphore_signal(barrier, inc=1, device_id=(column, row), device_id_type=MESH)

    load = pltpu.make_async_copy(input_ref, state_ref, load_sem)
    load.start()
    if nx == 2:
        around(greet)
        greetings = 2 * ny - 1
    else:

        @pl.when(at_edge)
        def _():
            around(greet)

        @pl.when(jnp.logical_not(at_edge))
        def _():
            greet(cx, up)
            greet(cx, down)

        @pl.when(jnp.logical_not(at_lower))
        def _():
            for row in near_rows:
                greet(cx - 1, row)

        @pl.when(jnp.logical_not(at_upper))
        def _():
            for row in near_rows:
                greet(cx + 1, row)

        greetings = jnp.where(at_edge, 2 * ny - 1 + 3, 2 + 6)

    lane = lax.broadcasted_iota(jnp.int32, (8, lanes), 1)
    sub = lane % 8
    part = lane // 8
    sublane = lax.broadcasted_iota(jnp.int32, (8, lanes), 0)
    swapped = lambda p: jnp.where(sub < 4, turned(p, -4, 1), turned(p, 4, 1))
    load.wait()
    tiles = []
    for t in (0, 8):
        packed = jnp.zeros((8, lanes), jnp.float32)
        for k in range(fields * depth):
            moved = turned(state_ref[k // depth, k % depth, t : t + 8, :], 8 * k + 4, 1)
            packed = jnp.where(part == k, moved, packed)
        tiles.append(packed)
    front = swapped(tiles[0])
    low = jnp.where(sub < 4, front, tiles[1])
    high = jnp.where(sub < 4, tiles[1], front)
    packs[0] = low
    packs[1] = high
    own_rows = pl.ds(pl.multiple_of(cy * 8, 8), 8)

    @pl.when(at_lower)
    def _():
        gather_low[own_rows, :] = low

    @pl.when(at_upper)
    def _():
        gather_high[own_rows, :] = high

    spots = []
    for k in range(fields * depth):
        f, z = k // depth, k % depth
        count = 3 if f == 6 else 2
        spots.append((spots[-1][0] + spots[-1][1] if spots else 0, count))
        rim_up[2 * k : 2 * k + 2, :] = state_ref[f, z, rows - 2 : rows, :]
        rim_down[spots[k][0] : spots[k][0] + count, :] = state_ref[f, z, 0:count, :]

    pl.semaphore_wait(barrier, greetings)

    def edge_copy(buffer, side, column, target, source):
        return pltpu.make_async_remote_copy(
            src_ref=packs.at[side],
            dst_ref=buffer.at[pl.ds(pl.multiple_of(source * 8, 8), 8), :],
            send_sem=send_edge.at[(column == cx).astype(jnp.int32), target],
            recv_sem=recv_edge.at[side, source],
            device_id=(column, target), device_id_type=MESH,
        )

    def side_copy(buffer, side, column, n):
        return pltpu.make_async_remote_copy(
            src_ref=packs.at[side], dst_ref=buffer.at[2 - n],
            send_sem=send_side.at[side, n], recv_sem=recv_side.at[side, 2 - n],
            device_id=(column, near_rows[n]), device_id_type=MESH,
        )

    def at_sides(method):
        @pl.when(at_lower)
        def _():
            around(lambda c, r: method(edge_copy(gather_low, 0, c, r, cy)))

        @pl.when(at_upper)
        def _():
            around(lambda c, r: method(edge_copy(gather_high, 1, c, r, cy)))

        @pl.when(jnp.logical_not(at_lower))
        def _():
            for n in range(3):
                method(side_copy(halo_right, 0, cx - 1, n))

        @pl.when(jnp.logical_not(at_upper))
        def _():
            for n in range(3):
                method(side_copy(halo_left, 1, cx + 1, n))

    def arrivals(wait):
        def from_edge(c, r):
            @pl.when(c == 0)
            def _():
                wait(edge_copy(gather_low, 0, c, r, r))

            @pl.when(c != 0)
            def _():
                wait(edge_copy(gather_high, 1, c, r, r))

        @pl.when(at_edge)
        def _():
            around(from_edge)

        @pl.when(jnp.logical_not(at_upper))
        def _():
            for n in range(3):
                wait(side_copy(halo_right, 0, cx + 1, 2 - n))

        @pl.when(jnp.logical_not(at_lower))
        def _():
            for n in range(3):
                wait(side_copy(halo_left, 1, cx - 1, 2 - n))

    rims = [
        pltpu.make_async_remote_copy(
            src_ref=rim_up, dst_ref=rim_low.at[pl.ds(8, 2 * fields * depth), :],
            send_sem=send_rim.at[0], recv_sem=recv_rim.at[0],
            device_id=(cx, up), device_id_type=MESH,
        ),
        pltpu.make_async_remote_copy(
            src_ref=rim_down, dst_ref=rim_high,
            send_sem=send_rim.at[1], recv_sem=recv_rim.at[1],
            device_id=(cx, down), device_id_type=MESH,
        ),
    ]
    at_sides(lambda copy: copy.start())
    for copy in rims:
        copy.start()
    arrivals(lambda copy: copy.wait_recv())
    for copy in rims:
        copy.wait_recv()

    def unfold(low, high):
        return jnp.where(sub < 4, low, high), swapped(jnp.where(sub < 4, high, low))

    total_rows = rows * ny

    def lay(block):
        a, b = unfold(gather_low[pl.ds(block * 8, 8), :], gather_high[pl.ds(block * 8, 8), :])
        joined[pl.ds(block * rows, 8), :] = a
        joined[pl.ds(block * rows + 8, 8), :] = b

    if ny > 16:
        lax.fori_loop(0, ny, lambda b, _: (lay(b), 0)[1], 0)
    else:
        for block in range(ny):
            lay(block)
    joined[total_rows : total_rows + 8, :] = joined[0:8, :]

    first, second = offsets_ref[0], offsets_ref[1]
    base = cy * rows

    def slab(shift):
        def part_at(j):
            return joined[pl.ds(lax.rem(base + shift + (j + 2 * total_rows), total_rows), 8), :]

        edge = jnp.where(sublane < 4, part_at(rows), part_at(-8))
        return [part_at(0), part_at(8), edge]

    field_of = part // depth

    def corrected(tiles, sign):
        along = jnp.where((field_of == 2) | (field_of == 4), sign * SHEAR_SPEED, 0.0)
        square = jnp.where(field_of == 4, 0.5 * SHEAR_SPEED * SHEAR_SPEED, 0.0)
        return [
            p + along * turned(p, 8 * 2 * depth, 1) + square * turned(p, 8 * 4 * depth, 1)
            for p in tiles
        ]

    side = lower_i - upper_i
    side_f = lower_f - upper_f
    sheared = corrected(slab(side * first), side_f)
    far = slab(side * second)
    near = corrected(slab(side * (second - first)), -side_f)
    beside = [unfold(halo_right[n], halo_left[n]) for n in range(3)]
    plain = [beside[1][0], beside[1][1], jnp.where(sublane < 4, beside[2][0], beside[0][1])]
    is_low = sub < 4
    from_shear = (is_low & at_upper) | (jnp.logical_not(is_low) & at_lower)
    ghosts = [jnp.where(from_shear, a, b) for a, b in zip(sheared, plain)]
    joint = [swapped(jnp.where(is_low == at_upper, a, b)) for a, b in zip(far, near)]

    stack = lambda tiles: jnp.concatenate(tiles, axis=0)
    ghosts, joint = stack(ghosts), stack(joint)
    height = rows + 8
    wide = lax.broadcasted_iota(jnp.int32, (height, lanes), 1)
    main, strip = [], []
    for f in range(8):
        main.append([])
        strip.append([])
        for z in range(depth):
            k = f * depth + z
            after, before = spots[k][0], 2 * k + 2
            edge = jnp.where(
                sublane < 4, rim_high[after : after + 8, :], rim_low[before : before + 8, :]
            )
            m = jnp.concatenate([state_ref[f, z], edge], axis=0)
            s = jnp.where(wide < 40, turned(m, 8, 1), m)
            s = jnp.where(wide < 8, turned(ghosts, -8 * k, 1), s)
            s = jnp.where((wide >= 40) & (wide < 48), turned(joint, 40 - 8 * k, 1), s)
            main[f].append(m)
            strip[f].append(s)

    main = advance(main, depth)
    strip = advance(strip, depth)
    back = jnp.where(at_lower, lanes - 36, lanes - 44)
    takes = ((wide == 7) & at_lower) | ((wide < 2) & at_upper)
    for z in range(depth):
        moved = [pltpu.roll(strip[f][z], back, 1) for f in range(8)]
        rho, my = moved[0], moved[2]
        moved[2] = my + (side_f * SHEAR_SPEED) * rho
        moved[4] = moved[4] + (side_f * SHEAR_SPEED) * my + (0.5 * SHEAR_SPEED * SHEAR_SPEED) * rho
        for f in range(8):
            strip[f][z] = jnp.where(takes, moved[f], strip[f][z])
    main = advance(main, depth)
    strip = advance(strip, depth)

    inner = wide[:rows]
    for f in range(8):
        for z in range(depth):
            s = strip[f][z][:rows]
            new = jnp.where(inner < 4, turned(s, -8, 1), jnp.where(inner >= lanes - 8, s, main[f][z][:rows]))
            out_ref[f, z] = 0.5 * (state_ref[f, z] + new)

    at_sides(lambda copy: copy.wait_send())
    for copy in rims:
        copy.wait_send()


def on_device(nx, ny, state, offsets):
    fields, depth, rows, lanes = state.shape
    dma = pltpu.SemaphoreType.DMA
    plane = lambda *sizes: pltpu.VMEM((*sizes, lanes), jnp.float32)
    lines = 2 * fields * depth
    return pl.pallas_call(
        functools.partial(kernel, nx, ny),
        out_shape=jax.ShapeDtypeStruct(state.shape, state.dtype),
        in_specs=[
            pl.BlockSpec(memory_space=pltpu.SMEM),
            pl.BlockSpec(memory_space=pl.ANY),
        ],
        out_specs=pl.BlockSpec(memory_space=pltpu.VMEM),
        scratch_shapes=[
            plane(fields, depth, rows), plane(2, 8),
            plane(lines), plane(lines + 8), plane(lines + 8), plane(lines + 8),
            plane(8 * ny), plane(8 * ny), plane(3, 8), plane(3, 8), plane(rows * ny + 8),
            dma((2, ny)), dma((2, ny)), dma((2, 3)), dma((2, 3)), dma((2,)), dma((2,)),
            dma,
        ],
        compiler_params=pltpu.CompilerParams(collective_id=0, has_side_effects=True),
    )(offsets, state)


def solution(mesh):
    nx, ny = mesh.shape["gx"], mesh.shape["gy"]
    return jax.shard_map(
        functools.partial(on_device, nx, ny),
        mesh=mesh,
        in_specs=(P(None, None, "gy", "gx"), P()),
        out_specs=P(None, None, "gy", "gx"),
        check_vma=False,
    )
```

time: 21 us -> 17.5 us (0.83)
  Pallas kernels: 19.3 us -> 15.8 us
    pallas_call x1, Pallas kernels: 19.3 us -> 15.8 us  [on_device(): pl.pallas_call(functools.partial(kernel, nx, ny), out_shape=jax.ShapeDtyp...]
where the time goes in v2:
time: 17.5 us; the launch traced here: 17.4 us
  Pallas kernels  15.8 us (90%)
  local copies, waits for them, and re-layouts  1.57 us (9%)
    pallas_call x1, Pallas kernels, on_device(): pl.pallas_call(functools.partial(kernel, nx, ny), out_shape=jax.ShapeDtyp...  15.8 us
    unnamed x1, local copies, waits for them, and re-layouts  1.57 us

profile of v2, /device:TPU:0, one launch (start us, length us, event | category | flops | bytes accessed | tf_op | source)
XLA Modules:
  0.0 17.4 jit_solution(9551625159430433960)
XLA Ops:
  0.0 15.8 %shard_map.28 = f32[8,2,16,128]{3,2,1,0:T(8,128)} custom-call(s32[2]{0:T(128)} %offsets_ref.1, f32[8,2,16,128]{3,2,1,0:T(8,128)} %input_ref.1), custom_call_target="tpu_custom_call" | custom-call | tf_op jit(solution)/shard_map/pallas_call | solution.py:386
  15.8 1.6 %copy.4 = f32[8,2,16,128]{3,2,1,0:T(8,128)} copy(f32[8,2,16,128]{3,2,1,0:T(8,128)} %shard_map.28) | data formatting | bytes 262144

commit v3 on v2

--- a/solution.py
+++ b/solution.py
@@ -275,12 +275,29 @@
             device_id=(cx, down), device_id_type=MESH,
         ),
     ]
+    for copy in rims:
+        copy.start()
     at_sides(lambda copy: copy.start())
     for copy in rims:
-        copy.start()
+        copy.wait_recv()
+
+    height = rows + 8
+    wide = lax.broadcasted_iota(jnp.int32, (height, lanes), 1)
+    whole = []
+    for f in range(fields):
+        whole.append([])
+        for z in range(depth):
+            after, before = spots[f * depth + z][0], 2 * (f * depth + z) + 2
+            edge = jnp.where(
+                sublane < 4, rim_high[after : after + 8, :], rim_low[before : before + 8, :]
+            )
+            whole[f].append(jnp.concatenate([state_ref[f, z], edge], axis=0))
+    main = advance(advance(whole, depth), depth)
+    for f in range(fields):
+        for z in range(depth):
+            out_ref[f, z] = 0.5 * (state_ref[f, z] + main[f][z][:rows])
+
     arrivals(lambda copy: copy.wait_recv())
-    for copy in rims:
-        copy.wait_recv()
 
     def unfold(low, high):
         return jnp.where(sub < 4, low, high), swapped(jnp.where(sub < 4, high, low))
@@ -333,11 +350,8 @@
 
     stack = lambda tiles: jnp.concatenate(tiles, axis=0)
     ghosts, joint = stack(ghosts), stack(joint)
-    height = rows + 8
-    wide = lax.broadcasted_iota(jnp.int32, (height, lanes), 1)
-    main, strip = [], []
-    for f in range(8):
-        main.append([])
+    strip = []
+    for f in range(fields):
         strip.append([])
         for z in range(depth):
             k = f * depth + z
@@ -349,10 +363,8 @@
             s = jnp.where(wide < 40, turned(m, 8, 1), m)
             s = jnp.where(wide < 8, turned(ghosts, -8 * k, 1), s)
             s = jnp.where((wide >= 40) & (wide < 48), turned(joint, 40 - 8 * k, 1), s)
-            main[f].append(m)
             strip[f].append(s)
 
-    main = advance(main, depth)
     strip = advance(strip, depth)
     back = jnp.where(at_lower, lanes - 36, lanes - 44)
     takes = ((wide == 7) & at_lower) | ((wide < 2) & at_upper)
@@ -363,15 +375,15 @@
         moved[4] = moved[4] + (side_f * SHEAR_SPEED) * my + (0.5 * SHEAR_SPEED * SHEAR_SPEED) * rho
         for f in range(8):
             strip[f][z] = jnp.where(takes, moved[f], strip[f][z])
-    main = advance(main, depth)
     strip = advance(strip, depth)
 
     inner = wide[:rows]
     for f in range(8):
         for z in range(depth):
             s = strip[f][z][:rows]
-            new = jnp.where(inner < 4, turned(s, -8, 1), jnp.where(inner >= lanes - 8, s, main[f][z][:rows]))
-            out_ref[f, z] = 0.5 * (state_ref[f, z] + new)
+            new = 0.5 * (state_ref[f, z] + jnp.where(inner < 4, turned(s, -8, 1), s))
+            keep = (inner >= 4) & (inner < lanes - 8)
+            out_ref[f, z] = jnp.where(keep, out_ref[f, z], new)
 
     at_sides(lambda copy: copy.wait_send())
     for copy in rims:

time: 17.5 us -> 16.1 us (0.920)
  Pallas kernels: 15.8 us -> 14.3 us
    pallas_call x1, Pallas kernels: 15.8 us -> 14.3 us  [on_device(): pl.pallas_call(functools.partial(kernel, nx, ny), out_shape=jax.ShapeDtyp...]
where the time goes in v3:
time: 16.1 us; the launch traced here: 15.9 us
  Pallas kernels  14.3 us (89%)
  local copies, waits for them, and re-layouts  1.57 us (10%)
    pallas_call x1, Pallas kernels, on_device(): pl.pallas_call(functools.partial(kernel, nx, ny), out_shape=jax.ShapeDtyp...  14.3 us
    unnamed x1, local copies, waits for them, and re-layouts  1.57 us

profile of v3, /device:TPU:0, one launch (start us, length us, event | category | flops | bytes accessed | tf_op | source)
XLA Modules:
  0.0 15.9 jit_solution(13924848144533669520)
XLA Ops:
  0.0 14.3 %shard_map.28 = f32[8,2,16,128]{3,2,1,0:T(8,128)} custom-call(s32[2]{0:T(128)} %offsets_ref.1, f32[8,2,16,128]{3,2,1,0:T(8,128)} %input_ref.1), custom_call_target="tpu_custom_call" | custom-call | tf_op jit(solution)/shard_map/pallas_call | solution.py:398
  14.4 1.6 %copy.4 = f32[8,2,16,128]{3,2,1,0:T(8,128)} copy(f32[8,2,16,128]{3,2,1,0:T(8,128)} %shard_map.28) | data formatting | bytes 262144

commit v4 on v3

--- a/solution.py
+++ b/solution.py
@@ -390,14 +390,20 @@
         copy.wait_send()
 
 
+def write_out(new_ref, out_ref, sem):
+    copy = pltpu.make_async_copy(new_ref, out_ref, sem)
+    copy.start()
+    copy.wait()
+
+
 def on_device(nx, ny, state, offsets):
     fields, depth, rows, lanes = state.shape
     dma = pltpu.SemaphoreType.DMA
     plane = lambda *sizes: pltpu.VMEM((*sizes, lanes), jnp.float32)
     lines = 2 * fields * depth
-    return pl.pallas_call(
+    new = pl.pallas_call(
         functools.partial(kernel, nx, ny),
-        out_shape=jax.ShapeDtypeStruct(state.shape, state.dtype),
+        out_shape=pltpu.VMEM(state.shape, state.dtype),
         in_specs=[
             pl.BlockSpec(memory_space=pltpu.SMEM),
             pl.BlockSpec(memory_space=pl.ANY),
@@ -410,8 +416,18 @@
             dma((2, ny)), dma((2, ny)), dma((2, 3)), dma((2, 3)), dma((2,)), dma((2,)),
             dma,
         ],
-        compiler_params=pltpu.CompilerParams(collective_id=0, has_side_effects=True),
+        compiler_params=pltpu.CompilerParams(
+            collective_id=0, has_side_effects=True
+        ),
     )(offsets, state)
+    return pl.pallas_call(
+        write_out,
+        out_shape=jax.ShapeDtypeStruct(state.shape, state.dtype),
+        in_specs=[pl.BlockSpec(memory_space=pltpu.VMEM)],
+        out_specs=pl.BlockSpec(memory_space=pl.ANY),
+        scratch_shapes=[dma],
+        compiler_params=pltpu.CompilerParams(vmem_limit_bytes=1 << 20),
+    )(new)
 
 
 def solution(mesh):

time: 16.1 us -> 14.5 us (0.901)
  local copies, waits for them, and re-layouts: 1.57 us -> 0 us
    unnamed x1 -> x0, local copies, waits for them, and re-layouts: 1.57 us -> none
    pallas_call x1 -> x2, Pallas kernels: 14.3 us -> 14.4 us  [the longest x1 13.7 us: on_device(): pl.pallas_call(functools.partial(kernel, nx, ny), out_shape=pltpu.VMEM(st...]
where the time goes in v4:
time: 14.5 us; the launch traced here: 14.4 us
  Pallas kernels  14.4 us (99%)
    pallas_call x1, Pallas kernels, on_device(): pl.pallas_call(functools.partial(kernel, nx, ny), out_shape=pltpu.VMEM(st...  13.7 us
    pallas_call x1, Pallas kernels, on_device(): pl.pallas_call(write_out, out_shape=jax.ShapeDtypeStruct(state.shape, sta...  0.67 us

profile of v4, /device:TPU:0, one launch (start us, length us, event | category | flops | bytes accessed | tf_op | source)
XLA Modules:
  0.0 14.4 jit_solution(17704408902291294530)
XLA Ops:
  0.0 13.7 %shard_map.28.new_ref = f32[8,2,16,128]{3,2,1,0:T(8,128)S(1)} custom-call(s32[2]{0:T(128)} %offsets_ref.1, f32[8,2,16,128]{3,2,1,0:T(8,128)} %input_ref.1), custom_call_target="tpu_custom_call" | custom-call | tf_op jit(solution)/shard_map/pallas_call | solution.py:404
  13.7 0.7 %shard_map.29 = f32[8,2,16,128]{3,2,1,0:T(8,128)} custom-call(f32[8,2,16,128]{3,2,1,0:T(8,128)S(1)} %shard_map.28.new_ref), custom_call_target="tpu_custom_call" | custom-call | tf_op jit(solution)/shard_map/pallas_call | solution.py:423

commit v5 on v4

--- a/solution.py
+++ b/solution.py
@@ -97,7 +97,7 @@
 
 def kernel(
     nx, ny, offsets_ref, input_ref, out_ref, state_ref, packs, rim_up, rim_down, rim_low, rim_high,
-    gather_low, gather_high, halo_left, halo_right, joined,
+    gather, halo, joined,
     send_edge, recv_edge, send_side, recv_side, send_rim, recv_rim, load_sem,
 ):
     fields, depth, rows, lanes = state_ref.shape
@@ -112,6 +112,8 @@
     upper_f = at_upper.astype(jnp.float32)
     opposite = jnp.where(at_lower, nx - 1, 0)
     near_rows = (down, cy, up)
+    outer = jnp.where(at_lower, 0, 1)
+    inner_side = 1 - outer
 
     def around(action):
         def step(d, _):
@@ -186,13 +188,7 @@
     packs[1] = high
     own_rows = pl.ds(pl.multiple_of(cy * 8, 8), 8)
 
-    @pl.when(at_lower)
-    def _():
-        gather_low[own_rows, :] = low
-
-    @pl.when(at_upper)
-    def _():
-        gather_high[own_rows, :] = high
+    gather[outer, own_rows, :] = jnp.where(at_lower, low, high)
 
     spots = []
     for k in range(fields * depth):
@@ -204,64 +200,53 @@
 
     pl.semaphore_wait(barrier, greetings)
 
-    def edge_copy(buffer, side, column, target, source):
+    def edge_copy(column, target):
         return pltpu.make_async_remote_copy(
-            src_ref=packs.at[side],
-            dst_ref=buffer.at[pl.ds(pl.multiple_of(source * 8, 8), 8), :],
-            send_sem=send_edge.at[(column == cx).astype(jnp.int32), target],
-            recv_sem=recv_edge.at[side, source],
+            src_ref=packs.at[outer], dst_ref=gather.at[outer, own_rows, :],
+            send_sem=send_edge, recv_sem=recv_edge.at[outer],
             device_id=(column, target), device_id_type=MESH,
         )
 
-    def side_copy(buffer, side, column, n):
+    def edge_wait(buffer, blocks, sem):
+        area = buffer.at[pl.ds(0, 8 * blocks), :]
+        pltpu.make_async_copy(area, area, sem).wait()
+
+    def side_copy(side, column, n):
         return pltpu.make_async_remote_copy(
-            src_ref=packs.at[side], dst_ref=buffer.at[2 - n],
+            src_ref=packs.at[side], dst_ref=halo.at[side, 2 - n],
             send_sem=send_side.at[side, n], recv_sem=recv_side.at[side, 2 - n],
             device_id=(column, near_rows[n]), device_id_type=MESH,
         )
 
-    def at_sides(method):
-        @pl.when(at_lower)
-        def _():
-            around(lambda c, r: method(edge_copy(gather_low, 0, c, r, cy)))
-
-        @pl.when(at_upper)
-        def _():
-            around(lambda c, r: method(edge_copy(gather_high, 1, c, r, cy)))
-
-        @pl.when(jnp.logical_not(at_lower))
-        def _():
+    def at_edges(action):
+        if nx == 2:
+            action()
+        else:
+            pl.when(at_edge)(action)
+
+    def sides(action, arriving):
+        if nx == 2:
             for n in range(3):
-                method(side_copy(halo_right, 0, cx - 1, n))
-
-        @pl.when(jnp.logical_not(at_upper))
-        def _():
-            for n in range(3):
-                method(side_copy(halo_left, 1, cx + 1, n))
-
-    def arrivals(wait):
-        def from_edge(c, r):
-            @pl.when(c == 0)
+                action(side_copy(outer if arriving else inner_side, opposite, n))
+            return
+        for side, column, absent in ((0, cx - 1, at_lower), (1, cx + 1, at_upper)):
+            if arriving:
+                column, absent = (cx + 1, at_upper) if side == 0 else (cx - 1, at_lower)
+
+            @pl.when(jnp.logical_not(absent))
             def _():
-                wait(edge_copy(gather_low, 0, c, r, r))
-
-            @pl.when(c != 0)
-            def _():
-                wait(edge_copy(gather_high, 1, c, r, r))
-
-        @pl.when(at_edge)
-        def _():
-            around(from_edge)
-
-        @pl.when(jnp.logical_not(at_upper))
-        def _():
-            for n in range(3):
-                wait(side_copy(halo_right, 0, cx + 1, 2 - n))
-
-        @pl.when(jnp.logical_not(at_lower))
-        def _():
-            for n in range(3):
-                wait(side_copy(halo_left, 1, cx - 1, 2 - n))
+                for n in range(3):
+                    action(side_copy(side, column, n))
+
+    def start_edges():
+        around(lambda column, row: edge_copy(column, row).start())
+
+    def await_edges():
+        edge_wait(gather.at[outer], ny - 1, recv_edge.at[outer])
+        edge_wait(gather.at[inner_side], ny, recv_edge.at[inner_side])
+
+    def await_sent_edges():
+        edge_wait(joined, 2 * ny - 1, send_edge)
 
     rims = [
         pltpu.make_async_remote_copy(
@@ -277,7 +262,8 @@
     ]
     for copy in rims:
         copy.start()
-    at_sides(lambda copy: copy.start())
+    at_edges(start_edges)
+    sides(lambda copy: copy.start(), False)
     for copy in rims:
         copy.wait_recv()
 
@@ -297,7 +283,12 @@
         for z in range(depth):
             out_ref[f, z] = 0.5 * (state_ref[f, z] + main[f][z][:rows])
 
-    arrivals(lambda copy: copy.wait_recv())
+    own_part = [
+        [jnp.where(wide < 40, turned(m, 8, 1), m) for m in levels] for levels in whole
+    ]
+
+    sides(lambda copy: copy.wait_recv(), True)
+    at_edges(await_edges)
 
     def unfold(low, high):
         return jnp.where(sub < 4, low, high), swapped(jnp.where(sub < 4, high, low))
@@ -305,7 +296,7 @@
     total_rows = rows * ny
 
     def lay(block):
-        a, b = unfold(gather_low[pl.ds(block * 8, 8), :], gather_high[pl.ds(block * 8, 8), :])
+        a, b = unfold(gather[0, pl.ds(block * 8, 8), :], gather[1, pl.ds(block * 8, 8), :])
         joined[pl.ds(block * rows, 8), :] = a
         joined[pl.ds(block * rows + 8, 8), :] = b
 
@@ -341,7 +332,7 @@
     sheared = corrected(slab(side * first), side_f)
     far = slab(side * second)
     near = corrected(slab(side * (second - first)), -side_f)
-    beside = [unfold(halo_right[n], halo_left[n]) for n in range(3)]
+    beside = [unfold(halo[0, n], halo[1, n]) for n in range(3)]
     plain = [beside[1][0], beside[1][1], jnp.where(sublane < 4, beside[2][0], beside[0][1])]
     is_low = sub < 4
     from_shear = (is_low & at_upper) | (jnp.logical_not(is_low) & at_lower)
@@ -355,12 +346,7 @@
         strip.append([])
         for z in range(depth):
             k = f * depth + z
-            after, before = spots[k][0], 2 * k + 2
-            edge = jnp.where(
-                sublane < 4, rim_high[after : after + 8, :], rim_low[before : before + 8, :]
-            )
-            m = jnp.concatenate([state_ref[f, z], edge], axis=0)
-            s = jnp.where(wide < 40, turned(m, 8, 1), m)
+            s = own_part[f][z]
             s = jnp.where(wide < 8, turned(ghosts, -8 * k, 1), s)
             s = jnp.where((wide >= 40) & (wide < 48), turned(joint, 40 - 8 * k, 1), s)
             strip[f].append(s)
@@ -385,7 +371,8 @@
             keep = (inner >= 4) & (inner < lanes - 8)
             out_ref[f, z] = jnp.where(keep, out_ref[f, z], new)
 
-    at_sides(lambda copy: copy.wait_send())
+    at_edges(await_sent_edges)
+    sides(lambda copy: copy.wait_send(), False)
     for copy in rims:
         copy.wait_send()
 
@@ -412,8 +399,8 @@
         scratch_shapes=[
             plane(fields, depth, rows), plane(2, 8),
             plane(lines), plane(lines + 8), plane(lines + 8), plane(lines + 8),
-            plane(8 * ny), plane(8 * ny), plane(3, 8), plane(3, 8), plane(rows * ny + 8),
-            dma((2, ny)), dma((2, ny)), dma((2, 3)), dma((2, 3)), dma((2,)), dma((2,)),
+            plane(2, 8 * ny), plane(2, 3, 8), plane(rows * ny + 8),
+            dma, dma((2,)), dma((2, 3)), dma((2, 3)), dma((2,)), dma((2,)),
             dma,
         ],
         compiler_params=pltpu.CompilerParams(

time: 14.5 us -> 13.7 us (0.945)
  Pallas kernels: 14.4 us -> 13.6 us
    pallas_call x1, Pallas kernels: 13.7 us -> 12.9 us  [on_device(): pl.pallas_call(functools.partial(kernel, nx, ny), out_shape=pltpu.VMEM(st...]
where the time goes in v5:
time: 13.7 us; the launch traced here: 13.6 us
  Pallas kernels  13.6 us (99%)
    pallas_call x1, Pallas kernels, on_device(): pl.pallas_call(functools.partial(kernel, nx, ny), out_shape=pltpu.VMEM(st...  12.9 us
    pallas_call x1, Pallas kernels, on_device(): pl.pallas_call(write_out, out_shape=jax.ShapeDtypeStruct(state.shape, sta...  0.67 us

profile of v5, /device:TPU:0, one launch (start us, length us, event | category | flops | bytes accessed | tf_op | source)
XLA Modules:
  0.0 13.6 jit_solution(15152994622271387519)
XLA Ops:
  0.0 12.9 %shard_map.28.new_ref = f32[8,2,16,128]{3,2,1,0:T(8,128)S(1)} custom-call(s32[2]{0:T(128)} %offsets_ref.1, f32[8,2,16,128]{3,2,1,0:T(8,128)} %input_ref.1), custom_call_target="tpu_custom_call" | custom-call | tf_op jit(solution)/shard_map/pallas_call | solution.py:391
  12.9 0.7 %shard_map.29 = f32[8,2,16,128]{3,2,1,0:T(8,128)} custom-call(f32[8,2,16,128]{3,2,1,0:T(8,128)S(1)} %shard_map.28.new_ref), custom_call_target="tpu_custom_call" | custom-call | tf_op jit(solution)/shard_map/pallas_call | solution.py:410
